TPU v7x, 128 devices: a whole 4x4x4 slice. The times are simulated.
128 devices in a mesh: seq: 32 (over z, x, core), head: 4 (over y).
Axes of the slice: x: 4, y: 4, z: 4, core: 2. Of those that a mesh axis runs over, the one named last changes fastest.
Arguments:
- queries: bfloat16 [16384, 4096], P('seq', 'head'), may hold values from -24 to 24
- key_states: bfloat16 [16384, 4096], P('seq', 'head'), may hold values from -24 to 24
- value_states: bfloat16 [16384, 4096], P('seq', 'head'), may hold values from -6 to 6
- forward_out: bfloat16 [16384, 4096], P('seq', 'head'), may hold values from -3 to 3
- grad_out: bfloat16 [16384, 4096], P('seq', 'head'), may hold values from -96 to 96
- random_blocks: int32 [256, 32, 3], P(None, 'head'), may hold values from 0 to 255, as said below
- global_blocks: int32 [2], replicated, may hold values from 0 to 255, as said below
Outputs:
- grad_queries: bfloat16 [16384, 4096], P(('seq', 'head'))
- grad_keys: bfloat16 [16384, 4096], P(('seq', 'head'))
- grad_values: bfloat16 [16384, 4096], P(('seq', 'head'))
Inputs may be any that keep to these rules, and one draw needn't show every extreme that they name: `random_blocks`: for the query blocks of one shard of 512 tokens and the 8 heads of one head group, at most 8 of the 192 entries name blocks held by any one shard of 8 blocks, and one shard, the same for every group, is named exactly 8 times by every group. `global_blocks`: two different blocks, one of them the last block 255.
All inputs are finite; a program needn't handle non-finite values.
Results may differ from a plain program's by a relative error of at most 0.0053.
Values may be sent and summed in bfloat16 or wider, within the bound.
A program may use at most 128 MiB of HBM per device.

v0:
```python
from functools import partial
import jax
import jax.numpy as jnp
from jax import lax
from jax.sharding import PartitionSpec as P

DH = 128
BS = 64


def padded(cells, sides, width):
    for axis, dim in sides:
        count = lax.axis_size(axis)
        ends = count - 1
        head = lax.slice_in_dim(cells, 0, width, axis=dim)
        tail = lax.slice_in_dim(cells, cells.shape[dim] - width, cells.shape[dim], axis=dim)
        cells = jnp.concatenate(
            [
                lax.ppermute(tail, axis, [(i, (i + 1) % count) for i in range(ends)]),
                cells,
                lax.ppermute(head, axis, [((i + 1) % count, i) for i in range(ends)]),
            ],
            axis=dim,
        )
    return cells


def scaled(values):
    return values * DH ** (-0.5)


def attend(
    query_row_block,
    gradient_row_block,
    saved_rows,
    gathered_key_block,
    gathered_value_block,
    usable,
    outer_max,
    outer_sum,
):
    logit_scores = scaled(
        jnp.einsum(
            "zxp,zufp->zxuf",
            query_row_block,
            gathered_key_block,
            preferred_element_type=jnp.float32,
        )
    )
    logit_scores = jnp.where(usable[:, None, :, None], logit_scores, -jnp.inf)
    peak_score = jnp.maximum(jnp.max(logit_scores, axis=(2, 3)), outer_max)
    row_sum = jnp.sum(jnp.exp(logit_scores - peak_score[:, :, None, None]), axis=(2, 3))
    row_sum = row_sum + outer_sum * jnp.exp(outer_max - peak_score)
    log_norm = peak_score + jnp.log(row_sum)
    weights = jnp.exp(logit_scores - log_norm[:, :, None, None])
    row_dot = jnp.sum(
        gradient_row_block.astype(jnp.float32) * saved_rows.astype(jnp.float32), axis=-1
    )
    weight_gradient = jnp.einsum(
        "zxp,zufp->zxuf",
        gradient_row_block,
        gathered_value_block,
        preferred_element_type=jnp.float32,
    )
    dscores = weights * (weight_gradient - row_dot[:, :, None, None])
    weight_lowp = weights.astype(jnp.bfloat16)
    score_gradient_lowp = dscores.astype(jnp.bfloat16)
    dq_terms = scaled(
        jnp.einsum(
            "bqjk,bjkd->bqjd",
            score_gradient_lowp,
            gathered_key_block,
            preferred_element_type=jnp.float32,
        )
    )
    key_gradient_parts = scaled(
        jnp.einsum(
            "rmnf,rmc->rnfc",
            score_gradient_lowp,
            query_row_block,
            preferred_element_type=jnp.float32,
        )
    )
    value_gradient_parts = jnp.einsum(
        "rmnf,rmc->rnfc", weight_lowp, gradient_row_block, preferred_element_type=jnp.float32
    )
    return (log_norm, row_dot, dq_terms, key_gradient_parts, value_gradient_parts)


def head_pass(operands, usable):
    (
        query_row_block,
        gradient_row_block,
        saved_rows,
        wide_keys,
        wide_values,
        glob_keys,
        glob_values,
        far_keys,
        far_values,
        outer_max,
        outer_sum,
    ) = operands
    block_count = query_row_block.shape[0]

    def listed(wide_rows, glob_rows, far_rows):
        window_set = jnp.stack([wide_rows[:-2], wide_rows[1:-1], wide_rows[2:]], axis=1)
        glob_set = jnp.broadcast_to(glob_rows[None], (block_count,) + glob_rows.shape)
        return jnp.concatenate([window_set, glob_set, far_rows], axis=1)

    log_norm, row_dot, dq_terms, key_gradient_parts, value_gradient_parts = attend(
        query_row_block,
        gradient_row_block,
        saved_rows,
        listed(wide_keys, glob_keys, far_keys),
        listed(wide_values, glob_values, far_values),
        usable,
        outer_max,
        outer_sum,
    )
    far_query = lax.optimization_barrier(dq_terms[:, :, 5:].astype(jnp.bfloat16)).astype(
        jnp.float32
    )
    grad_query = jnp.sum(dq_terms[:, :, :5], axis=2) + jnp.sum(far_query, axis=2)

    def spread(slot_terms):
        widths = ((0, 0), (0, 0), (0, 0))
        first = jnp.pad(slot_terms[:, 0], ((0, 2),) + widths[1:])
        middle = jnp.pad(slot_terms[:, 1], ((1, 1),) + widths[1:])
        last_part = jnp.pad(slot_terms[:, 2], ((2, 0),) + widths[1:])
        return first + middle + last_part

    return (
        grad_query,
        log_norm,
        row_dot,
        spread(key_gradient_parts),
        spread(value_gradient_parts),
        jnp.sum(key_gradient_parts[:, 3:5], axis=0),
        jnp.sum(value_gradient_parts[:, 3:5], axis=0),
        key_gradient_parts[:, 5:].astype(jnp.bfloat16),
        value_gradient_parts[:, 5:].astype(jnp.bfloat16),
    )


def on_device(
    queries, key_states, value_states, forward_out, grad_out, random_blocks, global_blocks
):
    seq_count = lax.axis_size("seq")
    my_seq = lax.axis_index("seq")
    tokens = queries.shape[0]
    blocks = tokens // BS
    head_count = queries.shape[1] // DH
    requests = blocks * head_count * 3
    slot_count = max(2, (5 * requests + 4 * seq_count - 1) // (4 * seq_count))
    kv_pair = jnp.stack([key_states, value_states])
    kv_wide = padded(kv_pair, (("seq", 1),), BS)
    kv_heads = kv_wide.reshape(2, blocks + 2, BS, head_count, DH).transpose(0, 3, 1, 2, 4)
    kv_owned = kv_heads[:, :, 1:-1]
    kv_flat = (
        kv_pair.reshape(2, blocks, BS, head_count, DH)
        .transpose(0, 1, 3, 2, 4)
        .reshape(2, blocks * head_count, BS, DH)
    )
    glob_owner = global_blocks // blocks
    glob_local = global_blocks % blocks
    glob_mine = glob_owner == my_seq
    picked = kv_owned[:, :, glob_local] * glob_mine.astype(jnp.bfloat16)[None, None, :, None, None]
    glob_kv = lax.psum(picked, "seq").astype(jnp.float32).astype(jnp.bfloat16)
    table = random_blocks.reshape(seq_count, requests)
    owner_of = table // blocks
    local_of = table % blocks
    seq_ids = jnp.arange(seq_count, dtype=jnp.int32)
    onehot = (owner_of[:, :, None] == seq_ids[None, None, :]).astype(jnp.int32)
    before = jnp.cumsum(onehot, axis=1) - onehot
    rank_of = jnp.sum(before * onehot, axis=2)
    my_owner = lax.dynamic_index_in_dim(owner_of, my_seq, 0, keepdims=False)
    my_rank = lax.dynamic_index_in_dim(rank_of, my_seq, 0, keepdims=False)
    send_pos = my_owner * slot_count + my_rank
    request_ids = jnp.arange(requests, dtype=jnp.int32)
    pair_of = request_ids // 3
    spill_slot = seq_count * slot_count
    target = jnp.where(
        owner_of == my_seq, seq_ids[:, None] * slot_count + rank_of, spill_slot
    ).reshape(-1)
    head_all = jnp.broadcast_to(pair_of % head_count, (seq_count, requests)).reshape(-1)
    recv_block = (
        jnp.zeros((spill_slot + 1,), jnp.int32).at[target].set(local_of.reshape(-1))[:spill_slot]
    )
    recv_head = jnp.zeros((spill_slot + 1,), jnp.int32).at[target].set(head_all)[:spill_slot]
    recv_used = jnp.zeros((spill_slot + 1,), jnp.float32).at[target].set(1.0)[:spill_slot]
    recv_index = recv_block * head_count + recv_head

    def head_major(array):
        return array.reshape(blocks, BS, head_count, DH).transpose(2, 0, 1, 3)

    query_heads = head_major(queries)
    grad_heads = head_major(grad_out)
    saved_heads = head_major(forward_out)
    block_ids = jnp.arange(blocks)
    always = jnp.ones((blocks,), bool)
    has_prev = (block_ids > 0) | (my_seq > 0)
    has_next = (block_ids < blocks - 1) | (my_seq < seq_count - 1)
    outgoing = kv_flat[:, recv_index]
    incoming = lax.all_to_all(outgoing, "seq", split_axis=1, concat_axis=1, tiled=True)
    fetched = (
        incoming[:, send_pos].reshape(2, blocks, head_count, 3, BS, DH).transpose(0, 2, 1, 3, 4, 5)
    )
    usable = jnp.stack([has_prev, always, has_next, always, always, always, always, always], axis=1)
    outer_max = jnp.full((head_count, blocks, BS), -jnp.inf, jnp.float32)
    outer_sum = jnp.zeros((head_count, blocks, BS), jnp.float32)
    results = lax.map(
        partial(head_pass, usable=usable),
        (
            query_heads,
            grad_heads,
            saved_heads,
            kv_heads[0],
            kv_heads[1],
            glob_kv[0],
            glob_kv[1],
            fetched[0],
            fetched[1],
            outer_max,
            outer_sum,
        ),
    )
    grad_query = results[0]
    far_pack = (
        jnp.stack([results[7], results[8]]).transpose(0, 2, 1, 3, 4, 5).reshape(2, requests, BS, DH)
    )
    sendback = jnp.zeros((2, spill_slot, BS, DH), jnp.bfloat16).at[:, send_pos].set(far_pack)
    returned = lax.all_to_all(sendback, "seq", split_axis=1, concat_axis=1, tiled=True)
    far_grads = returned.astype(jnp.float32) * recv_used[None, :, None, None]
    owned_far = (
        jnp.zeros((2, blocks * head_count, BS, DH), jnp.float32).at[:, recv_index].add(far_grads)
    )
    rim_pack = jnp.stack([results[3], results[4]])
    rim_out = jnp.concatenate([rim_pack[:, :, 0], rim_pack[:, :, -1]], axis=2)
    rim_in = padded(rim_out, (("seq", 2),), BS)
    owned = rim_pack[:, :, 1:-1]
    owned = owned.at[:, :, 0].add(rim_in[:, :, :BS]).at[:, :, -1].add(rim_in[:, :, -BS:])
    glob_sum = lax.psum(jnp.stack([results[5], results[6]]), "seq")
    glob_sum = glob_sum * glob_mine.astype(jnp.float32)[None, None, :, None, None]
    owned = owned.at[:, :, glob_local].add(glob_sum)
    owned = owned + owned_far.reshape(2, blocks, head_count, BS, DH).transpose(0, 2, 1, 3, 4)
    grads_kv = (
        owned.astype(jnp.bfloat16).transpose(0, 2, 3, 1, 4).reshape(2, tokens, head_count * DH)
    )
    dq_rows = grad_query.astype(jnp.bfloat16).transpose(1, 2, 0, 3).reshape(tokens, head_count * DH)
    out_query, out_keys, out_values = (
        lax.all_to_all(dq_rows, "head", split_axis=0, concat_axis=1, tiled=True),
        lax.all_to_all(grads_kv[0], "head", split_axis=0, concat_axis=1, tiled=True),
        lax.all_to_all(grads_kv[1], "head", split_axis=0, concat_axis=1, tiled=True),
    )
    return (out_query, out_keys, out_values)


def solution(mesh):
    return jax.shard_map(
        on_device,
        mesh=mesh,
        in_specs=(
            P("seq", "head"),
            P("seq", "head"),
            P("seq", "head"),
            P("seq", "head"),
            P("seq", "head"),
            P(None, "head", None),
            P(),
        ),
        out_specs=(P(("seq", "head"), None), P(("seq", "head"), None), P(("seq", "head"), None)),
        check_vma=False,
    )
```

profile of v0, /device:TPU:2, one launch (start us, length us, event | category | flops | bytes accessed | tf_op | source)
XLA Modules:
  0.0 855.4 jit_solution(16249413253305519232)
XLA Ops:
  10.5 18.4 %reduce-window.6 = s32[32,32,2,128]{3,1,2,0:T(8,128)S(1)} reduce-window(s32[32,32,2,128]{3,1,2,0:T(8,128)S(1)} %copy_bitcast_fusion.1, s32[]{:T(128)} %constant.212.clone.1), window={size=1x1x1x128 pad=0_0x0_0x0_0x127_0}, to_apply=%region_1.2 | reduce-window | flops 33292288 | bytes 2097156 | tf_op jit(solution)/shard_map/reduce-window
  31.0 23.0 %scatter_custom_fusion = s32[257]{0:T(512)S(1)} fusion(s32[6144]{0:T(1024)S(1)} %bitcast.346, s32[6144]{0:T(1024)S(1)} %add_select_fusion.1, s32[]{:T(128)} %constant.212.clone.1), kind=kCustom, calls=%fused_computation.170 | custom fusion | bytes 1032 | tf_op jit(solution)/shard_map/scatter | solution.py:188
  54.0 23.0 %scatter_custom_fusion.1 = s32[257]{0:T(512)S(1)} fusion(s32[6144]{0:T(1024)S(1)} %bitcast.347, s32[6144]{0:T(1024)S(1)} %reshape.454, s32[]{:T(128)} %constant.212.clone.1), kind=kCustom, calls=%fused_computation.168 | custom fusion | bytes 1032 | tf_op jit(solution)/shard_map/scatter | solution.py:190
  78.3 8.6 %gather_fusion.1 = bf16[256,2,64,128]{3,2,1,0:T(8,128)(2,1)} fusion(bf16[2,64,64,128]{3,2,1,0:T(8,128)(2,1)S(1)} %bitcast.306, s32[1024]{0:T(1024)S(1)} %pad_clamp_fusion.1), kind=kCustom, calls=%fused_computation.1 | custom fusion | bytes 16778240 | tf_op jit(solution)/shard_map/gather | solution.py:204
  87.0 8.6 %all-to-all-start = ((bf16[2,256,64,128]{3,2,0,1:T(8,128)(2,1)}), bf16[2,256,64,128]{3,2,0,1:T(8,128)(2,1)}, u32[]{:S(2)}, u32[]{:S(2)}) async-start(bf16[2,256,64,128]{3,2,0,1:T(8,128)(2,1)} %bitcast.307), calls=%async_computation | async-start | bytes 16777216 | tf_op jit(solution)/shard_map/all_to_all | solution.py:205
  117.1 76.9 %collective-permute-done = bf16[2,64,1024]{2,1,0:T(8,128)(2,1)S(1)} collective-permute-done((bf16[2,64,1024]{2,1,0:T(8,128)(2,1)}, bf16[2,64,1024]{2,1,0:T(8,128)(2,1)S(1)}, u32[]{:S(2)}, u32[]{:S(2)}) %collective-permute-start) | collective-permute-done | bytes 262176 | tf_op jit(solution)/shard_map/ppermute | solution.py:19
  206.1 107.6 %all-reduce.10.cloned.1.call-done = bf16[2,8,2,64,128]{4,3,1,0,2:T(8,128)(2,1)} async-done(((bf16[2,8,2,64,128]{4,3,1,0,2:T(8,128)(2,1)}), bf16[2,8,2,64,128]{4,3,1,0,2:T(8,128)(2,1)}) %all-reduce.10.cloned.1.call-update) | async-done | bytes 524304 | tf_op jit(solution)/shard_map/psum | solution.py:169
  314.7 11.5 %gather_fusion.2 = bf16[192,2,64,128]{3,2,1,0:T(8,128)(2,1)} fusion(bf16[2,256,64,128]{3,2,0,1:T(8,128)(2,1)} %all-to-all-done, s32[1024]{0:T(1024)S(1)} %pad_clamp_fusion), kind=kCustom, calls=%fused_computation.2 | custom fusion | bytes 12583680 | tf_op jit(solution)/shard_map/gather | solution.py:207
  326.2 4.3 copy.126
  334.7 149.4 %while.26 = (s32[]{:T(128)}, bf16[8,8,64,128]{3,2,1,0:T(8,128)(2,1)S(1)}, f32[8,10,64,128]{3,2,0,1:T(8,128)}, f32[8,10,64,128]{3,2,0,1:T(8,128)}, f32[8,2,64,128...) while((s32[]{:T(128)}, ...), condition=%wide.region_14.15_spmd, body=%wide.region_6.14_spmd.sunk | while | flops 340951552 | bytes 32071516 | solution.py:212
  492.0 5.5 broadcast_in_dim.140
  497.5 29.1 %scatter_fusion = bf16[2,256,64,128]{3,2,1,0:T(8,128)(2,1)} fusion(bf16[2,256,64,128]{3,2,1,0:T(8,128)(2,1)} %broadcast_in_dim.140, s32[192]{0:T(256)S(1)} %bitcast.350, bf16[192,2,64,128]{3,2,1,0:T(8,128)(2,1)} %copy.142), kind=kCustom, calls=%fused_computation.5 | custom fusion | bytes 18875136 | tf_op jit(solution)/shard_map/scatter | solution.py:232
  526.5 9.7 %copy.143 = bf16[2,256,64,128]{3,2,0,1:T(8,128)(2,1)} copy(bf16[2,256,64,128]{3,2,1,0:T(8,128)(2,1)} %scatter_fusion) | data formatting | bytes 16777216 | tf_op jit(solution)/shard_map/scatter | solution.py:232
  536.2 6.7 all-to-all-start.2
  550.2 96.7 %collective-permute-done.2 = f32[2,8,64,128]{3,2,1,0:T(8,128)} collective-permute-done((f32[2,8,64,128]{3,2,1,0:T(8,128)}, f32[2,8,64,128]{3,2,1,0:T(8,128)}, u32[]{:S(2)}, u32[]{:S(2)}) %collective-permute-start.2) | collective-permute-done | bytes 524320 | tf_op jit(solution)/shard_map/ppermute | solution.py:19
  652.0 23.0 %scatter_custom_fusion.3 = f32[257]{0:T(512)S(1)} fusion(s32[6144]{0:T(1024)S(1)} %bitcast.348, f32[6144]{0:T(1024)S(1)} %broadcast.368, f32[]{:T(128)} %constant.213.clone.1), kind=kCustom, calls=%fused_computation.166 | custom fusion | bytes 1032 | tf_op jit(solution)/shard_map/scatter | solution.py:191
  678.2 40.5 %all-reduce.12.cloned.1.call-done = f32[2,8,2,64,128]{4,3,2,1,0:T(8,128)} async-done(((f32[2,8,2,64,128]{4,3,2,1,0:T(8,128)}), f32[2,8,2,64,128]{4,3,2,1,0:T(8,128)}) %all-reduce.12.cloned.1.call-update) | async-done | bytes 1048592 | tf_op jit(solution)/shard_map/psum | solution.py:243
  724.3 4.5 all-to-all-start.1
  728.8 10.4 %multiply_bitcast_fusion.1 = f32[256,2,64,128]{3,2,1,0:T(8,128)} fusion(bf16[2,256,64,128]{3,2,0,1:T(8,128)(2,1)} %all-to-all-done.2, f32[256]{0:T(256)S(1)} %slice-done), kind=kLoop, calls=%fused_computation.73 | loop fusion | flops 8388608 | bytes 25166848 | tf_op jit(solution)/shard_map/mul | solution.py:234
  741.7 51.7 %scatter_fusion.1 = f32[2,64,64,128]{3,2,1,0:T(8,128)} fusion(f32[2,64,64,128]{3,2,1,0:T(8,128)} %broadcast_in_dim.139, s32[256]{0:T(256)S(1)} %compare_select_fusion.6, f32[256,2,64,128]{3,2,1,0:T(8,128)} %multiply_bitcast_fusion.1), kind=kCustom, calls=%fused_computation.7 | custom fusion | flops 4194304 | bytes 50332672 | tf_op jit(solution)/shard_map/scatter-add | solution.py:236
  793.4 6.8 bitcast_add_fusion
  809.1 4.7 all-to-all-start.3
  817.0 11.7 %all-to-all-done.3 = bf16[4,128,1024]{2,1,0:T(8,128)(2,1)S(1)} async-done(((bf16[4,128,1024]{2,1,0:T(8,128)(2,1)}), bf16[4,128,1024]{2,1,0:T(8,128)(2,1)S(1)}, u32[]{:S(2)}, u32[]{:S(2)}) %all-to-all-start.3) | async-done | bytes 1048608 | tf_op jit(solution)/shard_map/all_to_all | solution.py:253
  837.8 8.5 all-to-all-done.4
  (389 shorter events, 247.6 us)
Async XLA Ops:
  29.0 48.0 %copy-start.5 = (bf16[512,1024]{1,0:T(8,128)(2,1)S(1)}, bf16[512,1024]{1,0:T(8,128)(2,1)}, u32[]{:S(2)}) copy-start(bf16[512,1024]{1,0:T(8,128)(2,1)} %param.14) | copy-start | bytes 3145732
  29.8 47.5 %copy-start.4 = (bf16[512,1024]{1,0:T(8,128)(2,1)S(1)}, bf16[512,1024]{1,0:T(8,128)(2,1)}, u32[]{:S(2)}) copy-start(bf16[512,1024]{1,0:T(8,128)(2,1)} %param.15) | copy-start | bytes 3145732
  87.0 8.7 %copy-start.6 = (bf16[512,1024]{1,0:T(8,128)(2,1)S(1)}, bf16[512,1024]{1,0:T(8,128)(2,1)}, u32[]{:S(2)}) copy-start(bf16[512,1024]{1,0:T(8,128)(2,1)} %param.14) | copy-start | bytes 3145732
  87.0 227.7 %all-to-all-start = ((bf16[2,256,64,128]{3,2,0,1:T(8,128)(2,1)}), bf16[2,256,64,128]{3,2,0,1:T(8,128)(2,1)}, u32[]{:S(2)}, u32[]{:S(2)}) async-start(bf16[2,256,64,128]{3,2,0,1:T(8,128)(2,1)} %bitcast.307), calls=%async_computation | async-start | bytes 16777216 | tf_op jit(solution)/shard_map/all_to_all | solution.py:205
  95.6 6.5 copy-start.9
  95.6 218.0 %all-reduce.10.cloned.1.call-start = ((), (), s32[]{:S(2)}) async-start(), calls=%async_computation.5 | async-start | bytes 1048576 | tf_op jit(solution)/shard_map/psum | solution.py:169
  96.6 97.4 %collective-permute-start = (bf16[2,64,1024]{2,1,0:T(8,128)(2,1)}, bf16[2,64,1024]{2,1,0:T(8,128)(2,1)S(1)}, u32[]{:S(2)}, u32[]{:S(2)}) collective-permute-start(bf16[2,64,1024]{2,1,0:T(8,128)(2,1)} %get-tuple-element.381), channel_id=1, source_target_pairs={{0,4},{4,8},{8,12},{12,16},{16,20},{20,24},{24,28},{28,32},{32,36}... | collective-permute-start | bytes 786440 | tf_op jit(solution)/shard_map/ppermute | solution.py:19
  98.6 97.4 %collective-permute-start.1 = (bf16[2,64,1024]{2,1,0:T(8,128)(2,1)}, bf16[2,64,1024]{2,1,0:T(8,128)(2,1)}, u32[]{:S(2)}, u32[]{:S(2)}) collective-permute-start(bf16[2,64,1024]{2,1,0:T(8,128)(2,1)} %get-tuple-element.382), channel_id=1, source_target_pairs={{4,0},{8,4},{12,8},{16,12},{20,16},{24,20},{28,24},{32,28},{36,32}... | collective-permute-start | bytes 786440 | tf_op jit(solution)/shard_map/ppermute | solution.py:21
  102.2 5.0 copy-start.16
  330.5 4.2 copy-start.11
  330.5 4.2 copy-start.13
  484.1 3.8 copy-start.12
  536.2 6.8 copy-start
  536.2 188.1 %all-to-all-start.2 = ((bf16[2,256,64,128]{3,2,0,1:T(8,128)(2,1)}), bf16[2,256,64,128]{3,2,0,1:T(8,128)(2,1)}, u32[]{:S(2)}, u32[]{:S(2)}) async-start(bf16[2,256,64,128]{3,2,0,1:T(8,128)(2,1)} %copy.143), calls=%async_computation.2 | async-start | bytes 16777216 | tf_op jit(solution)/shard_map/all_to_all | solution.py:233
  543.0 175.7 %all-reduce.12.cloned.1.call-start = ((), (), s32[]{:S(2)}) async-start(), calls=%async_computation.6 | async-start | bytes 2097152 | tf_op jit(solution)/shard_map/psum | solution.py:243
  543.0 3.9 copy-start.14
  544.9 102.0 %collective-permute-start.2 = (f32[2,8,64,128]{3,2,1,0:T(8,128)}, f32[2,8,64,128]{3,2,1,0:T(8,128)}, u32[]{:S(2)}, u32[]{:S(2)}) collective-permute-start(f32[2,8,64,128]{3,2,1,0:T(8,128)} %fusion.31), channel_id=1, source_target_pairs={{0,4},{4,8},{8,12},{12,16},{16,20},{20,24},{24,28},{28,32},{32,36}... | collective-permute-start | bytes 1572872 | tf_op jit(solution)/shard_map/ppermute | solution.py:19
  548.0 98.9 %copy-start.1 = (f32[8,10,64,128]{3,2,0,1:T(8,128)S(1)}, f32[8,10,64,128]{3,2,0,1:T(8,128)}, u32[]{:S(2)}) copy-start(f32[8,10,64,128]{3,2,0,1:T(8,128)} %get-tuple-element.255) | copy-start | bytes 7864324
  650.1 73.4 %collective-permute-start.3 = (f32[2,8,64,128]{3,2,1,0:T(8,128)S(1)}, f32[2,8,64,128]{3,2,1,0:T(8,128)S(1)}, u32[]{:S(2)}, u32[]{:S(2)}) collective-permute-start(f32[2,8,64,128]{3,2,1,0:T(8,128)S(1)} %get-tuple-element.375), channel_id=1, source_target_pairs={{4,0},{8,4},{12,8},{16,12},{20,16},{24,20},{28,24},{32,28},{36,32}... | collective-permute-start | bytes 1572872 | tf_op jit(solution)/shard_map/ppermute | solution.py:21
  675.0 45.3 %copy-start.15 = (f32[257]{0:T(512)}, f32[257]{0:T(512)S(1)}, u32[]{:S(2)}) copy-start(f32[257]{0:T(512)S(1)} %scatter_custom_fusion.3) | copy-start | bytes 3088
  723.4 5.4 slice-start
  724.3 84.8 %all-to-all-start.1 = ((bf16[4,128,1024]{2,1,0:T(8,128)(2,1)}), bf16[4,128,1024]{2,1,0:T(8,128)(2,1)S(1)}, u32[]{:S(2)}, u32[]{:S(2)}) async-start(bf16[4,128,1024]{2,1,0:T(8,128)(2,1)} %all_to_all.49), calls=%async_computation.1 | async-start | bytes 2097152 | tf_op jit(solution)/shard_map/all_to_all | solution.py:252
  809.1 19.7 %all-to-all-start.3 = ((bf16[4,128,1024]{2,1,0:T(8,128)(2,1)}), bf16[4,128,1024]{2,1,0:T(8,128)(2,1)S(1)}, u32[]{:S(2)}, u32[]{:S(2)}) async-start(bf16[4,128,1024]{2,1,0:T(8,128)(2,1)} %all_to_all.54), calls=%async_computation.3 | async-start | bytes 2097152 | tf_op jit(solution)/shard_map/all_to_all | solution.py:253
  828.7 17.6 %all-to-all-start.4 = ((bf16[4,128,1024]{2,1,0:T(8,128)(2,1)}), bf16[4,128,1024]{2,1,0:T(8,128)(2,1)S(1)}, u32[]{:S(2)}, u32[]{:S(2)}) async-start(bf16[4,128,1024]{2,1,0:T(8,128)(2,1)} %all_to_all.58), calls=%async_computation.4 | async-start | bytes 2097152 | tf_op jit(solution)/shard_map/all_to_all | solution.py:254
  (5 other events, 15.8 us)
Sparse Core Ops, SparseCore 0:
  203.9 109.7 all-reduce.9
  548.1 170.5 all-reduce.11
where the time goes:
time: 868 us; the launch traced here: 855 us
  waiting for transfers between devices  344 us (40%)
  local copies, waits for them, and re-layouts  277 us (32%)
  other arithmetic  132 us (15%)
  matrix products  47.9 us (6%)
  starting transfers between devices  37.7 us (4%)
  between operations  14.9 us (2%)
    ppermute x2, waiting for transfers between devices, padded(): lax.ppermute(tail, axis, [(i, (i + 1) % count) for i in range(ends)])  174 us
    psum x1, waiting for transfers between devices, on_device(): glob_kv = lax.psum(picked, 'seq').astype(jnp.float32).astype(jnp.bfloat16)  108 us
    scatter-add x1, other arithmetic, on_device(): jnp.zeros((2, blocks * head_count, BS, DH), jnp.float32).at[:, recv_index]  51.7 us
    while x64, local copies, waits for them, and re-layouts  45.7 us
    psum x1, waiting for transfers between devices, on_device(): glob_sum = lax.psum(jnp.stack([results[5], results[6]]), 'seq')  40.5 us
    scatter x2, local copies, waits for them, and re-layouts, on_device(): jnp.zeros((2, spill_slot, BS, DH), jnp.bfloat16).at[:, send_pos]  38.8 us
    another operation x11, other arithmetic  25.8 us
    scatter x1, local copies, waits for them, and re-layouts, on_device(): jnp.zeros((spill_slot + 1,), jnp.int32).at[target].set(head_all)  23 us
  transfers between devices with their start and end apart: 11, of which 7 were waited for; matrix products, arithmetic and copies ran while one was open for 17% of the time, Pallas kernels for 0%

commit v1 on v0

--- a/solution.py
+++ b/solution.py
@@ -166,7 +166,9 @@
     glob_local = global_blocks % blocks
     glob_mine = glob_owner == my_seq
     picked = kv_owned[:, :, glob_local] * glob_mine.astype(jnp.bfloat16)[None, None, :, None, None]
-    glob_kv = lax.psum(picked, "seq").astype(jnp.float32).astype(jnp.bfloat16)
+    glob_kv = (
+        jnp.sum(lax.all_gather(picked, "seq"), axis=0).astype(jnp.float32).astype(jnp.bfloat16)
+    )
     table = random_blocks.reshape(seq_count, requests)
     owner_of = table // blocks
     local_of = table % blocks

time: 868 us -> 794 us (0.915)
  waiting for transfers between devices: 344 us -> 251 us
  other arithmetic: 132 us -> 156 us
  local copies, waits for them, and re-layouts: 277 us -> 261 us
    psum x1 -> x0, waiting for transfers between devices: 108 us -> none  [on_device(): glob_kv = lax.psum(picked, 'seq').astype(jnp.float32).astype(jnp.bfloat16)]
    all_to_all x1, waiting for transfers between devices: 0.01 us -> 91.9 us  [on_device(): lax.all_to_all(outgoing, 'seq', split_axis=1, concat_axis=1, tiled=True)]
    ppermute x2, waiting for transfers between devices: 174 us -> 97.6 us  [padded(): lax.ppermute(tail, axis, [(i, (i + 1) % count) for i in range(ends)])]
    while x64, local copies, waits for them, and re-layouts: 45.7 us -> 24 us
    another operation x11, other arithmetic: 25.8 us -> 40.6 us
    broadcast_in_dim x16, local copies, waits for them, and re-layouts: 0.19 us -> 12.3 us  [listed(): jnp.broadcast_to(glob_rows[None], (block_count,) + glob_rows.shape)]
    reduce_sum x0 -> x1, other arithmetic: none -> 9.15 us  [on_device(): jnp.sum(lax.all_gather(picked, 'seq'), axis=0).astype(jnp.float32)]
  transfers between devices with their start and end apart: 11 -> 11, of which waited for: 7 -> 7; matrix products, arithmetic and copies ran while one was open for 17% -> 32% of each run, Pallas kernels for 0% -> 0%
where the time goes in v1:
time: 794 us; the launch traced here: 779 us
  local copies, waits for them, and re-layouts  261 us (33%)
  waiting for transfers between devices  251 us (32%)
  other arithmetic  156 us (20%)
  matrix products  47.9 us (6%)
  starting transfers between devices  46.2 us (6%)
  between operations  14.9 us (2%)
    ppermute x2, waiting for transfers between devices, padded(): lax.ppermute(tail, axis, [(i, (i + 1) % count) for i in range(ends)])  97.6 us
    all_to_all x1, waiting for transfers between devices, on_device(): lax.all_to_all(outgoing, 'seq', split_axis=1, concat_axis=1, tiled=True)  91.9 us
    scatter-add x1, other arithmetic, on_device(): jnp.zeros((2, blocks * head_count, BS, DH), jnp.float32).at[:, recv_index]  51.8 us
    another operation x11, other arithmetic  40.6 us
    psum x1, waiting for transfers between devices, on_device(): glob_sum = lax.psum(jnp.stack([results[5], results[6]]), 'seq')  40.5 us
    scatter x2, local copies, waits for them, and re-layouts, on_device(): jnp.zeros((2, spill_slot, BS, DH), jnp.bfloat16).at[:, send_pos]  38.7 us
    while x64, local copies, waits for them, and re-layouts  24 us
    scatter x1, local copies, waits for them, and re-layouts, on_device(): jnp.zeros((spill_slot + 1,), jnp.float32).at[target].set(1.0)[:spill_slot]  23.2 us
  transfers between devices with their start and end apart: 11, of which 7 were waited for; matrix products, arithmetic and copies ran while one was open for 32% of the time, Pallas kernels for 0%

profile of v1, /device:TPU:2, one launch (start us, length us, event | category | flops | bytes accessed | tf_op | source)
XLA Modules:
  0.0 778.6 jit_solution(12713466689635118469)
XLA Ops:
  28.9 32.3 %reduce-window.6 = s32[32,32,2,128]{3,1,2,0:T(8,128)S(1)} reduce-window(s32[32,32,2,128]{3,1,2,0:T(8,128)} %copy_bitcast_fusion, s32[]{:T(128)} %constant.214.clone.1), window={size=1x1x1x128 pad=0_0x0_0x0_0x127_0}, to_apply=%region_1.2 | reduce-window | flops 33292288 | bytes 2097156 | tf_op jit(solution)/shard_map/reduce-window
  65.4 23.0 %scatter_custom_fusion = s32[257]{0:T(512)S(1)} fusion(s32[6144]{0:T(1024)S(1)} %bitcast.344, s32[6144]{0:T(1024)S(1)} %add_select_fusion.1, s32[]{:T(128)} %constant.214.clone.1), kind=kCustom, calls=%fused_computation.169 | custom fusion | bytes 1032 | tf_op jit(solution)/shard_map/scatter | solution.py:190
  88.4 23.0 %scatter_custom_fusion.1 = s32[257]{0:T(512)S(1)} fusion(s32[6144]{0:T(1024)S(1)} %bitcast.345, s32[6144]{0:T(1024)S(1)} %reshape.461, s32[]{:T(128)} %constant.214.clone.1), kind=kCustom, calls=%fused_computation.167 | custom fusion | bytes 1032 | tf_op jit(solution)/shard_map/scatter | solution.py:192
  112.7 8.6 %gather_fusion.1 = bf16[256,2,64,128]{3,2,1,0:T(8,128)(2,1)} fusion(bf16[2,64,64,128]{3,2,1,0:T(8,128)(2,1)S(1)} %bitcast.305, s32[1024]{0:T(1024)S(1)} %pad_clamp_fusion.1), kind=kCustom, calls=%fused_computation.1 | custom fusion | bytes 16778240 | tf_op jit(solution)/shard_map/gather | solution.py:206
  121.3 12.4 %all-to-all-start = ((bf16[2,256,64,128]{3,2,0,1:T(8,128)(2,1)}), bf16[2,256,64,128]{3,2,0,1:T(8,128)(2,1)}, u32[]{:S(2)}, u32[]{:S(2)}) async-start(bf16[2,256,64,128]{3,2,0,1:T(8,128)(2,1)} %bitcast.306), calls=%async_computation | async-start | bytes 16777216 | tf_op jit(solution)/shard_map/all_to_all | solution.py:207
  141.1 91.9 %all-to-all-done = bf16[2,256,64,128]{3,2,0,1:T(8,128)(2,1)} async-done(((bf16[2,256,64,128]{3,2,0,1:T(8,128)(2,1)}), bf16[2,256,64,128]{3,2,0,1:T(8,128)(2,1)}, u32[]{:S(2)}, u32[]{:S(2)}) %all-to-all-start) | async-done | bytes 8388640 | tf_op jit(solution)/shard_map/all_to_all | solution.py:207
  233.0 11.5 %gather_fusion.2 = bf16[192,2,64,128]{3,2,1,0:T(8,128)(2,1)} fusion(bf16[2,256,64,128]{3,2,0,1:T(8,128)(2,1)} %all-to-all-done, s32[1024]{0:T(1024)S(1)} %pad_clamp_fusion), kind=kCustom, calls=%fused_computation.2 | custom fusion | bytes 12583680 | tf_op jit(solution)/shard_map/gather | solution.py:209
  244.5 4.3 copy.125
  253.0 9.2 %reduce_sum.93 = bf16[2,8,2,64,128]{4,3,2,1,0:T(8,128)(2,1)S(1)} reduce(bf16[32,2,8,2,64,128]{5,4,3,2,1,0:T(8,128)(2,1)} %all-gather.2.cloned.1.call-done, bf16[]{:T(256)} %constant.216.clone.1), dimensions={0}, to_apply=%region_0.1 | reduce | flops 8126464 | bytes 17301506 | tf_op jit(solution)/shard_map/reduce_sum | solution.py:170
  263.0 139.8 %while.26 = (s32[]{:T(128)}, bf16[8,8,64,128]{3,2,1,0:T(8,128)(2,1)S(1)}, f32[8,10,64,128]{3,2,0,1:T(8,128)}, f32[8,10,64,128]{3,2,0,1:T(8,128)}, f32[8,2,64,128...) while((s32[]{:T(128)}, ...), condition=%wide.region_14.15_spmd, body=%wide.region_6.14_spmd.sunk | while | flops 340951552 | bytes 32071516 | solution.py:214
  410.8 5.4 broadcast_in_dim.140
  416.2 29.1 %scatter_fusion = bf16[2,256,64,128]{3,2,1,0:T(8,128)(2,1)} fusion(bf16[2,256,64,128]{3,2,1,0:T(8,128)(2,1)} %broadcast_in_dim.140, s32[192]{0:T(256)S(1)} %bitcast.348, bf16[192,2,64,128]{3,2,1,0:T(8,128)(2,1)} %copy.143), kind=kCustom, calls=%fused_computation.5 | custom fusion | bytes 18875136 | tf_op jit(solution)/shard_map/scatter | solution.py:234
  445.2 9.6 %copy.144 = bf16[2,256,64,128]{3,2,0,1:T(8,128)(2,1)} copy(bf16[2,256,64,128]{3,2,1,0:T(8,128)(2,1)} %scatter_fusion) | data formatting | bytes 16777216 | tf_op jit(solution)/shard_map/scatter | solution.py:234
  454.9 11.4 %all-to-all-start.2 = ((bf16[2,256,64,128]{3,2,0,1:T(8,128)(2,1)}), bf16[2,256,64,128]{3,2,0,1:T(8,128)(2,1)}, u32[]{:S(2)}, u32[]{:S(2)}) async-start(bf16[2,256,64,128]{3,2,0,1:T(8,128)(2,1)} %copy.144), calls=%async_computation.2 | async-start | bytes 16777216 | tf_op jit(solution)/shard_map/all_to_all | solution.py:235
  473.6 96.9 %collective-permute-done.2 = f32[2,8,64,128]{3,2,1,0:T(8,128)} collective-permute-done((f32[2,8,64,128]{3,2,1,0:T(8,128)}, f32[2,8,64,128]{3,2,1,0:T(8,128)}, u32[]{:S(2)}, u32[]{:S(2)}) %collective-permute-start.2) | collective-permute-done | bytes 524320 | tf_op jit(solution)/shard_map/ppermute | solution.py:19
  575.5 23.2 %scatter_custom_fusion.3 = f32[257]{0:T(512)S(1)} fusion(s32[6144]{0:T(1024)S(1)} %bitcast.346, f32[6144]{0:T(1024)S(1)} %broadcast.375, f32[]{:T(128)} %constant.215.clone.1), kind=kCustom, calls=%fused_computation.165 | custom fusion | bytes 1032 | tf_op jit(solution)/shard_map/scatter | solution.py:193
  601.9 40.5 %all-reduce.9.cloned.1.call-done = f32[2,8,2,64,128]{4,3,2,1,0:T(8,128)} async-done(((f32[2,8,2,64,128]{4,3,2,1,0:T(8,128)}), f32[2,8,2,64,128]{4,3,2,1,0:T(8,128)}) %all-reduce.9.cloned.1.call-update) | async-done | bytes 1048592 | tf_op jit(solution)/shard_map/psum | solution.py:245
  648.1 4.3 all-to-all-start.1
  652.4 10.3 %multiply_bitcast_fusion.1 = f32[256,2,64,128]{3,2,1,0:T(8,128)} fusion(bf16[2,256,64,128]{3,2,0,1:T(8,128)(2,1)} %all-to-all-done.2, f32[256]{0:T(256)S(1)} %slice-done), kind=kLoop, calls=%fused_computation.73 | loop fusion | flops 8388608 | bytes 25166848 | tf_op jit(solution)/shard_map/mul | solution.py:236
  665.1 51.8 %scatter_fusion.1 = f32[2,64,64,128]{3,2,1,0:T(8,128)} fusion(f32[2,64,64,128]{3,2,1,0:T(8,128)} %broadcast_in_dim.139, s32[256]{0:T(256)S(1)} %compare_select_fusion.6, f32[256,2,64,128]{3,2,1,0:T(8,128)} %multiply_bitcast_fusion.1), kind=kCustom, calls=%fused_computation.7 | custom fusion | flops 4194304 | bytes 50332672 | tf_op jit(solution)/shard_map/scatter-add | solution.py:238
  716.9 6.8 bitcast_add_fusion
  732.7 5.0 all-to-all-start.3
  740.9 11.4 %all-to-all-done.3 = bf16[4,128,1024]{2,1,0:T(8,128)(2,1)S(1)} async-done(((bf16[4,128,1024]{2,1,0:T(8,128)(2,1)}), bf16[4,128,1024]{2,1,0:T(8,128)(2,1)S(1)}, u32[]{:S(2)}, u32[]{:S(2)}) %all-to-all-start.3) | async-done | bytes 1048608 | tf_op jit(solution)/shard_map/all_to_all | solution.py:255
  761.4 8.2 %all-to-all-done.4 = bf16[4,128,1024]{2,1,0:T(8,128)(2,1)S(1)} async-done(((bf16[4,128,1024]{2,1,0:T(8,128)(2,1)}), bf16[4,128,1024]{2,1,0:T(8,128)(2,1)S(1)}, u32[]{:S(2)}, u32[]{:S(2)}) %all-to-all-start.4) | async-done | bytes 1048608 | tf_op jit(solution)/shard_map/all_to_all | solution.py:256
  (396 shorter events, 232.2 us)
Async XLA Ops:
  7.2 10.8 %copy-start.6 = (bf16[512,1024]{1,0:T(8,128)(2,1)S(1)}, bf16[512,1024]{1,0:T(8,128)(2,1)}, u32[]{:S(2)}) copy-start(bf16[512,1024]{1,0:T(8,128)(2,1)} %param.14) | copy-start | bytes 3145732
  7.2 10.8 %copy-start.7 = (bf16[512,1024]{1,0:T(8,128)(2,1)S(1)}, bf16[512,1024]{1,0:T(8,128)(2,1)}, u32[]{:S(2)}) copy-start(bf16[512,1024]{1,0:T(8,128)(2,1)} %param.15) | copy-start | bytes 3145732
  7.2 245.8 %all-gather.2.cloned.1.call-start = ((), (), s32[]{:S(2)}) async-start(), calls=%async_computation.5 | async-start | bytes 17301504 | tf_op jit(solution)/shard_map/all_gather | solution.py:170
  8.5 7.7 collective-permute-start
  10.4 7.5 collective-permute-start.1
  14.8 4.2 copy-start.17
  20.5 4.8 copy-start.15
  121.3 12.5 %copy-start.8 = (bf16[512,1024]{1,0:T(8,128)(2,1)S(1)}, bf16[512,1024]{1,0:T(8,128)(2,1)}, u32[]{:S(2)}) copy-start(bf16[512,1024]{1,0:T(8,128)(2,1)} %param.13) | copy-start | bytes 3145732
  121.3 111.7 %all-to-all-start = ((bf16[2,256,64,128]{3,2,0,1:T(8,128)(2,1)}), bf16[2,256,64,128]{3,2,0,1:T(8,128)(2,1)}, u32[]{:S(2)}, u32[]{:S(2)}) async-start(bf16[2,256,64,128]{3,2,0,1:T(8,128)(2,1)} %bitcast.306), calls=%async_computation | async-start | bytes 16777216 | tf_op jit(solution)/shard_map/all_to_all | solution.py:207
  252.9 10.0 %copy-start.11 = (bf16[8,8,64,128]{3,2,1,0:T(8,128)(2,1)S(1)}, bf16[8,8,64,128]{3,2,1,0:T(8,128)(2,1)}, u32[]{:S(2)}) copy-start(bf16[8,8,64,128]{3,2,1,0:T(8,128)(2,1)} %custom-call.8) | copy-start | bytes 3145732
  454.9 11.5 %copy-start = (f32[8,10,64,128]{3,2,0,1:T(8,128)S(1)}, f32[8,10,64,128]{3,2,0,1:T(8,128)}, u32[]{:S(2)}) copy-start(f32[8,10,64,128]{3,2,0,1:T(8,128)} %get-tuple-element.256) | copy-start | bytes 7864324
  454.9 193.2 %all-to-all-start.2 = ((bf16[2,256,64,128]{3,2,0,1:T(8,128)(2,1)}), bf16[2,256,64,128]{3,2,0,1:T(8,128)(2,1)}, u32[]{:S(2)}, u32[]{:S(2)}) async-start(bf16[2,256,64,128]{3,2,0,1:T(8,128)(2,1)} %copy.144), calls=%async_computation.2 | async-start | bytes 16777216 | tf_op jit(solution)/shard_map/all_to_all | solution.py:235
  466.3 4.0 copy-start.13
  466.3 176.1 %all-reduce.9.cloned.1.call-start = ((), (), s32[]{:S(2)}) async-start(), calls=%async_computation.6 | async-start | bytes 2097152 | tf_op jit(solution)/shard_map/psum | solution.py:245
  466.4 3.9 copy-start.14
  468.2 102.2 %collective-permute-start.2 = (f32[2,8,64,128]{3,2,1,0:T(8,128)}, f32[2,8,64,128]{3,2,1,0:T(8,128)}, u32[]{:S(2)}, u32[]{:S(2)}) collective-permute-start(f32[2,8,64,128]{3,2,1,0:T(8,128)} %fusion.31), channel_id=1, source_target_pairs={{0,4},{4,8},{8,12},{12,16},{16,20},{20,24},{24,28},{28,32},{32,36}... | collective-permute-start | bytes 1572872 | tf_op jit(solution)/shard_map/ppermute | solution.py:19
  471.4 99.1 %copy-start.1 = (f32[8,10,64,128]{3,2,0,1:T(8,128)S(1)}, f32[8,10,64,128]{3,2,0,1:T(8,128)}, u32[]{:S(2)}) copy-start(f32[8,10,64,128]{3,2,0,1:T(8,128)} %get-tuple-element.255) | copy-start | bytes 7864324
  573.6 73.6 %collective-permute-start.3 = (f32[2,8,64,128]{3,2,1,0:T(8,128)S(1)}, f32[2,8,64,128]{3,2,1,0:T(8,128)S(1)}, u32[]{:S(2)}, u32[]{:S(2)}) collective-permute-start(f32[2,8,64,128]{3,2,1,0:T(8,128)S(1)} %get-tuple-element.375), channel_id=1, source_target_pairs={{4,0},{8,4},{12,8},{16,12},{20,16},{24,20},{28,24},{32,28},{36,32}... | collective-permute-start | bytes 1572872 | tf_op jit(solution)/shard_map/ppermute | solution.py:21
  598.7 45.3 %copy-start.16 = (f32[257]{0:T(512)}, f32[257]{0:T(512)S(1)}, u32[]{:S(2)}) copy-start(f32[257]{0:T(512)S(1)} %scatter_custom_fusion.3) | copy-start | bytes 3088
  647.2 5.2 slice-start
  648.1 84.6 %all-to-all-start.1 = ((bf16[4,128,1024]{2,1,0:T(8,128)(2,1)}), bf16[4,128,1024]{2,1,0:T(8,128)(2,1)S(1)}, u32[]{:S(2)}, u32[]{:S(2)}) async-start(bf16[4,128,1024]{2,1,0:T(8,128)(2,1)} %all_to_all.49), calls=%async_computation.1 | async-start | bytes 2097152 | tf_op jit(solution)/shard_map/all_to_all | solution.py:254
  716.9 6.8 copy-start.18
  732.7 19.6 %all-to-all-start.3 = ((bf16[4,128,1024]{2,1,0:T(8,128)(2,1)}), bf16[4,128,1024]{2,1,0:T(8,128)(2,1)S(1)}, u32[]{:S(2)}, u32[]{:S(2)}) async-start(bf16[4,128,1024]{2,1,0:T(8,128)(2,1)} %all_to_all.54), calls=%async_computation.3 | async-start | bytes 2097152 | tf_op jit(solution)/shard_map/all_to_all | solution.py:255
  752.3 17.2 %all-to-all-start.4 = ((bf16[4,128,1024]{2,1,0:T(8,128)(2,1)}), bf16[4,128,1024]{2,1,0:T(8,128)(2,1)S(1)}, u32[]{:S(2)}, u32[]{:S(2)}) async-start(bf16[4,128,1024]{2,1,0:T(8,128)(2,1)} %all_to_all.58), calls=%async_computation.4 | async-start | bytes 2097152 | tf_op jit(solution)/shard_map/all_to_all | solution.py:256
  (7 other events, 15.1 us)
Sparse Core Ops, SparseCore 0:
  25.4 78.1 all-gather.1
  471.5 170.8 all-reduce.8
